TPU v7x, 512 devices: a whole 4x4x16 slice. The times are simulated.
512 devices in a mesh: tok: 128 (over y, z_lo, x, core), head: 4 (over z_hi).
Axes of the slice: x: 4, y: 4, z: 16 (z_hi: 4, z_lo: 4; z = z_hi * 4 + z_lo), core: 2. Of those that a mesh axis runs over, the one named last changes fastest.
Arguments:
- fast_query: bfloat16 [2, 16384, 2048], P(None, 'tok', 'head'), may hold values from -6 to 6
- fast_key: bfloat16 [2, 16384, 2048], P(None, 'tok', 'head'), may hold values from -6 to 6
- fast_value: bfloat16 [2, 16384, 2048], P(None, 'tok', 'head'), may hold values from -6 to 6
- fast_rate: float32 [2, 16384, 4], P(None, 'tok', 'head'), may hold values from 0.00078125 to 0.0078125
- fast_weights: bfloat16 [4, 512, 3, 512], P('head', 'tok'), may hold values from -0.25 to 0.25
- norm_gain: float32 [2048], P('head'), may hold values from 0.25 to 1.75
- key_value: bfloat16 [2, 16384, 512], P(None, 'tok', 'head'), may hold values from -450 to 450
Outputs:
- layer_output: bfloat16 [2, 16384, 2048], P(None, 'tok', 'head')
All inputs are finite; a program needn't handle non-finite values.
Results may differ from a plain program's by a relative error of at most 0.04.
The roundings to bfloat16 on the way count: a program that leaves them out, or rounds other values in their place, can miss the bound.
Values may be sent and summed in bfloat16 or wider, within the bound.
No kernel may reach another device: no remote copies, remote signals or barrier semaphores. Data moves between devices by JAX's collectives and lax.ppermute only.
A program may use at most 64 MiB of HBM per device.

v0:
```python
import math

import jax
import jax.numpy as jnp
from jax import lax
from jax.sharding import PartitionSpec as P

WIN = 1024


EPSILON = 1e-06


def from_partner(block, axis, stride):
    count = lax.axis_size(axis)
    route = []
    for low in range(count):
        high = low | 1 << stride
        if high != low and high < count:
            route += [(low, high), (high, low)]
    return lax.ppermute(block, axis, route)


def passed_along(array, axis, by):
    length = lax.axis_size(axis)
    return lax.ppermute(array, axis, [(i, (i + by) % length) for i in range(length)])


def product(inputs, matrix):
    return jnp.dot(inputs, matrix, preferred_element_type=jnp.float32)


def fast_apply(inputs, weights):
    gate_value = product(inputs, weights[:, 0])
    up_value = product(inputs, weights[:, 1])
    hidden = (jax.nn.silu(gate_value) * up_value).astype(jnp.bfloat16)
    return product(hidden, weights[:, 2])


def backward_terms(key_in, value_in, rates, weights):
    gate_value = product(key_in, weights[:, 0])
    up_value = product(key_in, weights[:, 1])
    sigmoid_gate = jax.nn.sigmoid(gate_value)
    activated = gate_value * sigmoid_gate
    key_hidden = (activated * up_value).astype(jnp.bfloat16)
    scaled = (rates * value_in.astype(jnp.float32)).astype(jnp.bfloat16)
    backward = lax.dot_general(
        scaled, weights[:, 2], (((1,), (1,)), ((), ())), preferred_element_type=jnp.float32
    )
    gate_grad = (
        backward * up_value * sigmoid_gate * (1.0 + gate_value * (1.0 - sigmoid_gate))
    ).astype(jnp.bfloat16)
    up_grad = (backward * activated).astype(jnp.bfloat16)
    return (key_hidden, scaled, gate_grad, up_grad)


def gradient_rows(key_in, terms):
    key_hidden, scaled, gate_grad, up_grad = terms
    across = (((0,), (0,)), ((), ()))
    gate_rows = lax.dot_general(key_in, gate_grad, across, preferred_element_type=jnp.float32)
    up_rows = lax.dot_general(key_in, up_grad, across, preferred_element_type=jnp.float32)
    down_rows = lax.dot_general(key_hidden, scaled, across, preferred_element_type=jnp.float32)
    return jnp.stack([gate_rows, up_rows, down_rows], axis=1)


def renormed(previous, gradient):
    earlier = previous.astype(jnp.float32)
    updated = earlier + gradient
    factor = jnp.sqrt(jnp.mean(earlier * earlier, axis=-1, keepdims=True) + EPSILON) * lax.rsqrt(
        jnp.mean(updated * updated, axis=-1, keepdims=True) + EPSILON
    )
    return (updated * factor).astype(jnp.bfloat16)


def normalized(raw, gain_row):
    factor = lax.rsqrt(jnp.mean(raw * raw, axis=-1, keepdims=True) + EPSILON)
    return (raw * factor * gain_row).astype(jnp.bfloat16)


def attend(queries, key_block, value_block, allowed, head_size):
    tokens = queries.shape[0]
    per_head = queries.reshape(tokens, -1, head_size)
    scores = jnp.einsum(
        "qhd,kd->hqk", per_head, key_block, preferred_element_type=jnp.float32
    ) / math.sqrt(head_size)
    scores = jnp.where(allowed[None], scores, -1e30)
    row_max = jnp.max(scores, axis=-1, keepdims=True)
    lifted = jnp.exp(scores - row_max)
    weights = (lifted / jnp.sum(lifted, axis=-1, keepdims=True)).astype(jnp.bfloat16)
    mixed = jnp.einsum("hqk,kd->qhd", weights, value_block, preferred_element_type=jnp.float32)
    return mixed.reshape(tokens, -1)


def shards(fast_query, fast_key, fast_value, fast_rate, fast_weights, norm_gain, key_value):
    tokens = fast_query.shape[1]
    head_size = key_value.shape[2]
    place = lax.axis_index("tok")
    block_len = tokens * lax.axis_size("tok")
    own_rows = fast_weights[0]
    initial = lax.all_gather(own_rows, "tok", axis=0, tiled=True)
    terms = backward_terms(fast_key[0], fast_value[0], fast_rate[0], initial)
    gradient = lax.psum(gradient_rows(fast_key[0], terms), "tok")
    refreshed = renormed(initial, gradient)
    partner = from_partner(key_value, "head", 0)
    holds_key = lax.axis_index("head") % 2 == 0
    key_part = jnp.where(holds_key, key_value, partner)
    value_part = jnp.where(holds_key, partner, key_value)
    pair_stack = jnp.stack([key_part, value_part])
    reach = WIN // tokens
    arrived = []
    for distance in range(1, reach + 1):
        arrived.append(passed_along(pair_stack, "tok", distance))
    aligned = []
    for distance in range(reach, 0, -1):
        piece = arrived[distance - 1]
        aligned.append(jnp.where(place >= distance, piece, piece[:, 0:1]))
    aligned.append(pair_stack)
    window = jnp.concatenate(aligned, axis=2)
    span = window.shape[2]
    query_pos = lax.broadcasted_iota(jnp.int32, (tokens, span), 0)
    key_pos = lax.broadcasted_iota(jnp.int32, (tokens, span), 1) - reach * tokens
    offset = query_pos - key_pos
    inside = (offset >= 0) & (offset < WIN)

    def finish(block_index, matrices):
        fast_out = normalized(fast_apply(fast_query[block_index], matrices), norm_gain)
        allowed = inside & (block_index * block_len + place * tokens + key_pos >= 0)
        attended = attend(
            fast_out, window[0, block_index], window[1, block_index], allowed, head_size
        )
        return (fast_out.astype(jnp.float32) + attended).astype(jnp.bfloat16)

    first_final = finish(0, initial)
    second_final = finish(1, refreshed)
    return jnp.stack([first_final, second_final])


def solution(mesh):
    in_specs = (
        P(None, "tok", "head"),
        P(None, "tok", "head"),
        P(None, "tok", "head"),
        P(None, "tok", "head"),
        P("head", "tok", None, None),
        P("head"),
        P(None, "tok", "head"),
    )
    out_specs = P(None, "tok", "head")
    return jax.shard_map(shards, mesh=mesh, in_specs=in_specs, out_specs=out_specs, check_vma=False)
```

profile of v0, /device:TPU:1, one launch (start us, length us, event | category | flops | bytes accessed | tf_op | source)
XLA Modules:
  0.0 1575.3 jit_solution(1581133232713736569)
XLA Ops:
  6.5 1.3 copy.19
  7.9 9.6 collective-permute-start
  17.6 1.9 fusion.26
  19.5 0.9 select_bitcast_fusion.1
  20.4 4.2 collective-permute-start.1
  24.6 1.1 slice_bitcast_fusion.49
  25.7 6.0 collective-permute-start.2
  31.7 4.3 collective-permute-start.3
  36.0 4.2 collective-permute-start.4
  40.2 4.4 collective-permute-start.5
  44.6 5.0 collective-permute-start.6
  49.7 2.5 collective-permute-start.7
  52.2 1.9 collective-permute-start.8
  54.2 4.1 collective-permute-done.6
  58.3 3.1 collective-permute-done.7
  61.4 0.7 select_dynamic-update-slice_fusion.7
  62.1 162.6 %all-gather.3.cloned.1.call-done = bf16[1,512,3,512]{3,2,0,1:T(4,128)(2,1)} async-done(((bf16[1,4,3,512]{3,2,0,1:T(4,128)(2,1)}), bf16[1,512,3,512]{3,2,0,1:T(4,128)(2,1)}) %all-gather.3.cloned.1.call-update) | async-done | bytes 1572880 | tf_op jit(solution)/shard_map/all_gather | solution.py:100
  224.7 2.9 copy.20
  229.9 2.0 pad_maximum_fusion
  232.0 0.7 select_dynamic-update-slice_fusion.6
  232.6 0.7 select_dynamic-update-slice_fusion.5
  234.1 0.7 select_dynamic-update-slice_fusion.3
  234.8 0.7 select_dynamic-update-slice_fusion.2
  235.5 0.7 select_dynamic-update-slice_fusion.1
  238.8 1.9 fusion.124
  240.8 2.4 fusion.11
  243.3 1314.1 %all-reduce.2.cloned.1.call-done = f32[512,3,512]{0,2,1:T(8,128)} async-done(((f32[512,3,512]{0,2,1:T(8,128)}), f32[512,3,512]{0,2,1:T(8,128)}) %all-reduce.2.cloned.1.call-update) | async-done | bytes 3145744 | tf_op jit(solution)/shard_map/psum | solution.py:102
  1557.4 2.7 fusion.10
  1561.5 1.5 multiply_reduce_fusion.1
  1563.2 1.9 fusion.129
  1565.1 2.3 fusion.12
  1567.7 0.7 pad_maximum_fusion.1
  (68 shorter events, 7.6 us)
Async XLA Ops:
  6.5 218.1 %all-gather.3.cloned.1.call-start = ((), (), s32[]{:S(2)}) async-start(), calls=%async_computation.1 | async-start | bytes 2113536 | tf_op jit(solution)/shard_map/all_gather | solution.py:100
  7.9 1549.5 %all-reduce.2.cloned.1.call-start = ((), (), s32[]{:S(2)}) async-start(), calls=%async_computation | async-start | bytes 6291456 | tf_op jit(solution)/shard_map/psum | solution.py:102
  7.9 11.6 collective-permute-start
  20.4 24.2 %collective-permute-start.1 = (bf16[2,2,128,128]{3,2,1,0:T(8,128)(2,1)S(1)}, bf16[2,2,128,128]{3,2,1,0:T(8,128)(2,1)S(1)}, u32[]{:S(2)}, u32[]{:S(2)}) collective-permute-start(bf16[2,2,128,128]{3,2,1,0:T(8,128)(2,1)S(1)} %pad_maximum_fusion.2), channel_id=1, source_target_pairs={{0,32},{4,36},{8,40},{12,44},{16,48},{20,52},{24,56},{28,60},{32,6... | collective-permute-start | bytes 393224 | tf_op jit(solution)/shard_map/ppermute | solution.py:26
  25.7 24.0 %collective-permute-start.2 = (bf16[2,2,128,128]{3,2,1,0:T(8,128)(2,1)S(1)}, bf16[2,2,128,128]{3,2,1,0:T(8,128)(2,1)S(1)}, u32[]{:S(2)}, u32[]{:S(2)}) collective-permute-start(bf16[2,2,128,128]{3,2,1,0:T(8,128)(2,1)S(1)} %pad_maximum_fusion.2), channel_id=1, source_target_pairs={{0,28},{4,32},{8,36},{12,40},{16,44},{20,48},{24,52},{28,56},{32,6... | collective-permute-start | bytes 393224 | tf_op jit(solution)/shard_map/ppermute | solution.py:26
  31.7 20.5 %collective-permute-start.3 = (bf16[2,2,128,128]{3,2,1,0:T(8,128)(2,1)S(1)}, bf16[2,2,128,128]{3,2,1,0:T(8,128)(2,1)S(1)}, u32[]{:S(2)}, u32[]{:S(2)}) collective-permute-start(bf16[2,2,128,128]{3,2,1,0:T(8,128)(2,1)S(1)} %pad_maximum_fusion.2), channel_id=1, source_target_pairs={{0,24},{4,28},{8,32},{12,36},{16,40},{20,44},{24,48},{28,52},{32,5... | collective-permute-start | bytes 393224 | tf_op jit(solution)/shard_map/ppermute | solution.py:26
  36.0 18.1 %collective-permute-start.4 = (bf16[2,2,128,128]{3,2,1,0:T(8,128)(2,1)S(1)}, bf16[2,2,128,128]{3,2,1,0:T(8,128)(2,1)S(1)}, u32[]{:S(2)}, u32[]{:S(2)}) collective-permute-start(bf16[2,2,128,128]{3,2,1,0:T(8,128)(2,1)S(1)} %pad_maximum_fusion.2), channel_id=1, source_target_pairs={{0,20},{4,24},{8,28},{12,32},{16,36},{20,40},{24,44},{28,48},{32,5... | collective-permute-start | bytes 393224 | tf_op jit(solution)/shard_map/ppermute | solution.py:26
  40.2 14.0 collective-permute-start.5
  44.6 13.7 collective-permute-start.6
  49.7 11.7 collective-permute-start.7
  52.2 179.7 %collective-permute-start.8 = (bf16[2,2,128,128]{3,2,1,0:T(8,128)(2,1)S(1)}, bf16[2,2,128,128]{3,2,1,0:T(8,128)(2,1)S(1)}, u32[]{:S(2)}, u32[]{:S(2)}) collective-permute-start(bf16[2,2,128,128]{3,2,1,0:T(8,128)(2,1)S(1)} %pad_maximum_fusion.2), channel_id=1, source_target_pairs={{0,4},{4,8},{8,12},{12,16},{16,20},{20,24},{24,28},{28,32},{32,36}... | collective-permute-start | bytes 393224 | tf_op jit(solution)/shard_map/ppermute | solution.py:26
  62.1 165.5 %copy-start.1 = (bf16[2,128,512]{2,1,0:T(8,128)(2,1)S(1)}, bf16[2,128,512]{2,1,0:T(8,128)(2,1)}, u32[]{:S(2)}) copy-start(bf16[2,128,512]{2,1,0:T(8,128)(2,1)} %param.8) | copy-start | bytes 786436
  227.6 1.0 copy-start.2
  227.6 0.9 copy-start.10
  231.9 5.7 copy-start.6
  237.9 0.9 copy-start.5
  237.9 0.9 copy-start.8
  238.5 2.2 copy-start.3
  238.5 2.2 copy-start.11
  1557.4 2.8 copy-start
  1560.2 0.9 copy-start.7
  1561.5 1.6 copy-start.4
  1561.5 1.6 copy-start.9
  1561.5 1.6 copy-start.12
Sparse Core Ops, SparseCore 0:
  9.5 215.1 all-gather.2
  232.0 1325.3 all-reduce.1
where the time goes:
time: 1580 us
  waiting for transfers between devices  1480 us (94%)
  starting transfers between devices  42.2 us (3%)
    psum x1, waiting for transfers between devices, shards(): gradient = lax.psum(gradient_rows(fast_key[0], terms), 'tok')  1310 us
    all_gather x1, waiting for transfers between devices, shards(): initial = lax.all_gather(own_rows, 'tok', axis=0, tiled=True)  163 us
    ppermute x8, starting transfers between devices, passed_along(): lax.ppermute(array, axis, [(i, (i + by) % length) for i in range(length)])  32.5 us
  transfers between devices with their start and end apart: 11, of which 4 were waited for; matrix products, arithmetic and copies ran while one was open for 1% of the time, Pallas kernels for 0%

commit v1 on v0

v1 whole, which is shorter than its diff:
```python
import math

import jax
import jax.numpy as jnp
from jax import lax
from jax.sharding import Mesh, PartitionSpec as P

WIN = 1024
EPSILON = 1e-06
TOK = ("y", "z", "x", "c")
PLANE = ("y", "x")


def product(inputs, matrix):
    return jnp.dot(inputs, matrix, preferred_element_type=jnp.float32)


def order_matrix(width):
    sizes = [lax.axis_size(axis) for axis in TOK]
    ny, nz, nx, nc = sizes
    nj = width // (ny * nz * nx * nc)
    place = lax.broadcasted_iota(jnp.int32, (width, width), 1)
    j = place % nj
    z = place // nj % nz
    x = place // (nj * nz) % nx
    y = place // (nj * nz * nx) % ny
    c = place // (nj * nz * nx * ny)
    natural = (((y * nz + z) * nx + x) * nc + c) * nj + j
    return (natural == lax.broadcasted_iota(jnp.int32, (width, width), 0)).astype(jnp.bfloat16)


def exchange(array, axes):
    return lax.all_to_all(array, axes, 0, 0)


def to_all(array, axes):
    count = lax.axis_size(axes)
    return exchange(jnp.broadcast_to(array[None], (count,) + array.shape), axes)


def other_core(array):
    return lax.ppermute(array, "c", [(0, 1), (1, 0)])


def halves(array, core):
    half = array.shape[1] // 2
    first, second = array[:, :half], array[:, half:]
    return jnp.where(core == 0, first, second), jnp.where(core == 0, second, first)


def against(pair, own, other, low, high):
    return product(pair[0], own[:, low:high]) + product(pair[1], other[:, low:high])


def fast_apply(pair, own, other, core, width):
    gate_value = against(pair, own, other, 0, width)
    up_value = against(pair, own, other, width, 2 * width)
    hidden = (jax.nn.silu(gate_value) * up_value).astype(jnp.bfloat16)
    return against(halves(hidden, core), own, other, 2 * width, 3 * width)


def gradient(pair, value_in, rates, own, other, core, width):
    gate_value = against(pair, own, other, 0, width)
    up_value = against(pair, own, other, width, 2 * width)
    sigmoid_gate = jax.nn.sigmoid(gate_value)
    activated = gate_value * sigmoid_gate
    key_hidden = (activated * up_value).astype(jnp.bfloat16)
    scaled = (rates * value_in.astype(jnp.float32)).astype(jnp.bfloat16)
    along = (((1,), (1,)), ((), ()))
    back_own = lax.dot_general(scaled, own[:, 2 * width:], along, preferred_element_type=jnp.float32)
    back_other = lax.dot_general(scaled, other[:, 2 * width:], along, preferred_element_type=jnp.float32)
    backward = jnp.concatenate(
        [jnp.where(core == 0, back_own, back_other), jnp.where(core == 0, back_other, back_own)], axis=1
    )
    gate_grad = (
        backward * up_value * sigmoid_gate * (1.0 + gate_value * (1.0 - sigmoid_gate))
    ).astype(jnp.bfloat16)
    up_grad = (backward * activated).astype(jnp.bfloat16)
    across = (((0,), (0,)), ((), ()))
    hidden_pair = halves(key_hidden, core)

    def rows(which):
        return jnp.concatenate([
            lax.dot_general(pair[which], gate_grad, across, preferred_element_type=jnp.float32),
            lax.dot_general(pair[which], up_grad, across, preferred_element_type=jnp.float32),
            lax.dot_general(hidden_pair[which], scaled, across, preferred_element_type=jnp.float32),
        ], axis=1)

    return rows(0), rows(1).astype(jnp.bfloat16)


def renormed(previous, total, width):
    count = previous.shape[0]
    earlier = previous.astype(jnp.float32).reshape(count, 3, width)
    updated = earlier + total.reshape(count, 3, width)
    factor = jnp.sqrt(jnp.mean(earlier * earlier, axis=-1, keepdims=True) + EPSILON) * lax.rsqrt(
        jnp.mean(updated * updated, axis=-1, keepdims=True) + EPSILON
    )
    return (updated * factor).astype(jnp.bfloat16).reshape(count, 3 * width)


def normalized(raw, gain_row):
    factor = lax.rsqrt(jnp.mean(raw * raw, axis=-1, keepdims=True) + EPSILON)
    return (raw * factor * gain_row).astype(jnp.bfloat16)


def attend(queries, key_block, value_block, allowed, head_size):
    tokens = queries.shape[0]
    per_head = queries.reshape(tokens, -1, head_size)
    scores = jnp.einsum(
        "qhd,kd->hqk", per_head, key_block, preferred_element_type=jnp.float32
    ) / math.sqrt(head_size)
    scores = jnp.where(allowed[None], scores, -1e30)
    row_max = jnp.max(scores, axis=-1, keepdims=True)
    lifted = jnp.exp(scores - row_max)
    weights = (lifted / jnp.sum(lifted, axis=-1, keepdims=True)).astype(jnp.bfloat16)
    mixed = jnp.einsum("hqk,kd->qhd", weights, value_block, preferred_element_type=jnp.float32)
    return mixed.reshape(tokens, -1)


def passed_along(array, by):
    length = lax.axis_size(TOK)
    return lax.ppermute(array, TOK, [(i, (i + by) % length) for i in range(length)])


def preceding(key_value, place, reach):
    count = lax.axis_size("head")
    partner = lax.ppermute(key_value, "head", [(i, i ^ 1) for i in range(count)])
    holds_key = lax.axis_index("head") % 2 == 0
    pair = jnp.stack([jnp.where(holds_key, key_value, partner), jnp.where(holds_key, partner, key_value)])
    runs = [pair]
    step = 1
    while len(runs) < reach + 1:
        part = jnp.stack(runs[:step])
        for k in (1, 2):
            if len(runs) < reach + 1:
                moved = passed_along(part, k * step)
                runs += [moved[i] for i in range(step)]
        step = len(runs)
    aligned = []
    for distance in range(reach, 0, -1):
        piece = runs[distance]
        aligned.append(jnp.where(place >= distance, piece, piece[:, 0:1]))
    aligned.append(pair)
    return jnp.concatenate(aligned, axis=2)


def shards(fast_query, fast_key, fast_value, fast_rate, fast_weights, norm_gain, key_value):
    tokens, width = fast_query.shape[1:]
    head_size = key_value.shape[2]
    place = lax.axis_index(TOK)
    core = lax.axis_index("c")
    block_len = tokens * lax.axis_size(TOK)
    reach = WIN // tokens

    order = order_matrix(width)

    def reordered(array):
        return product(array, order).astype(jnp.bfloat16)

    rows = fast_weights[0]
    count = rows.shape[0]
    sides = reordered(rows[:, :2].reshape(2 * count, width)).reshape(count, 2 * width)
    own_rows = jnp.concatenate([sides, rows[:, 2]], axis=1)
    base = to_all(own_rows, "z").reshape(-1, 3 * width)
    own = to_all(base, PLANE).reshape(-1, 3 * width)
    other = other_core(own)

    window = preceding(key_value, place, reach)

    mine, theirs = gradient(
        halves(reordered(fast_key[0]), core), fast_value[0], fast_rate[0], own, other, core, width
    )
    chip_sum = (mine + other_core(theirs).astype(jnp.float32)).astype(jnp.bfloat16)
    pieces = exchange(chip_sum.reshape((-1,) + base.shape), PLANE)
    plane_sum = jnp.sum(pieces.astype(jnp.float32), axis=0).astype(jnp.bfloat16)
    total = jnp.sum(to_all(plane_sum, "z").astype(jnp.float32), axis=0)
    new_rows = renormed(base, total, width)
    new_own = to_all(new_rows, PLANE).reshape(-1, 3 * width)
    new_other = other_core(new_own)

    span = window.shape[2]
    query_pos = lax.broadcasted_iota(jnp.int32, (tokens, span), 0)
    key_pos = lax.broadcasted_iota(jnp.int32, (tokens, span), 1) - reach * tokens
    offset = query_pos - key_pos
    inside = (offset >= 0) & (offset < WIN)

    def finish(block_index, matrices):
        pair = halves(reordered(fast_query[block_index]), core)
        fast_out = normalized(fast_apply(pair, *matrices, core, width), norm_gain)
        allowed = inside & (block_index * block_len + place * tokens + key_pos >= 0)
        attended = attend(fast_out, window[0, block_index], window[1, block_index], allowed, head_size)
        return (fast_out.astype(jnp.float32) + attended).astype(jnp.bfloat16)

    return jnp.stack([finish(0, (own, other)), finish(1, (new_own, new_other))])


def solution(mesh):
    heads = mesh.shape["head"]
    fine = Mesh(mesh.devices.reshape(4, 4, 4, 2, heads), TOK + ("head",))
    in_specs = (
        P(None, TOK, "head"),
        P(None, TOK, "head"),
        P(None, TOK, "head"),
        P(None, TOK, "head"),
        P("head", TOK, None, None),
        P("head"),
        P(None, TOK, "head"),
    )
    out_specs = P(None, TOK, "head")
    return jax.shard_map(shards, mesh=fine, in_specs=in_specs, out_specs=out_specs, check_vma=False)
```

time: 1580 us -> 147 us (0.09)
  waiting for transfers between devices: 1480 us -> 49.9 us
    psum x1 -> x0, waiting for transfers between devices: 1310 us -> none  [shards(): gradient = lax.psum(gradient_rows(fast_key[0], terms), 'tok')]
    all_gather x1 -> x0, waiting for transfers between devices: 163 us -> none  [shards(): initial = lax.all_gather(own_rows, 'tok', axis=0, tiled=True)]
    all_to_all x0 -> x5, waiting for transfers between devices: none -> 25.7 us  [exchange(): return lax.all_to_all(array, axes, 0, 0)]
    all_to_all x0 -> x5, starting transfers between devices: none -> 23 us  [exchange(): return lax.all_to_all(array, axes, 0, 0)]
    ppermute x9 -> x8, waiting for transfers between devices: 7.2 us -> 24.2 us  [the longest x4 22.7 us: passed_along(): lax.ppermute(array, TOK, [(i, (i + by) % length) for i in range(length)])]
    ppermute x9 -> x8, starting transfers between devices: 42.2 us -> 33.8 us  [the longest x4 14.6 us: passed_along(): lax.ppermute(array, TOK, [(i, (i + by) % length) for i in range(length)])]
  transfers between devices with their start and end apart: 11 -> 13, of which waited for: 4 -> 8; matrix products, arithmetic and copies ran while one was open for 1% -> 17% of each run, Pallas kernels for 0% -> 0%
where the time goes in v1:
time: 147 us; the launch traced here: 146 us
  starting transfers between devices  56.8 us (39%)
  waiting for transfers between devices  49.9 us (34%)
  matrix products  18.7 us (13%)
  other arithmetic  11 us (7%)
  local copies, waits for them, and re-layouts  8.78 us (6%)
    all_to_all x5, waiting for transfers between devices, exchange(): return lax.all_to_all(array, axes, 0, 0)  25.7 us
    all_to_all x5, starting transfers between devices, exchange(): return lax.all_to_all(array, axes, 0, 0)  23 us
    ppermute x4, waiting for transfers between devices, passed_along(): lax.ppermute(array, TOK, [(i, (i + by) % length) for i in range(length)])  22.7 us
    ppermute x4, starting transfers between devices, passed_along(): lax.ppermute(array, TOK, [(i, (i + by) % length) for i in range(length)])  14.6 us
    ppermute x3, starting transfers between devices, other_core(): return lax.ppermute(array, 'c', [(0, 1), (1, 0)])  10.4 us
    ppermute x1, starting transfers between devices, preceding(): lax.ppermute(key_value, 'head', [(i, i ^ 1) for i in range(count)])  8.81 us
    dot_general x20, matrix products, product(): return jnp.dot(inputs, matrix, preferred_element_type=jnp.float32)  8.09 us
    unnamed x8, other arithmetic  5.55 us
  transfers between devices with their start and end apart: 13, of which 8 were waited for; matrix products, arithmetic and copies ran while one was open for 17% of the time, Pallas kernels for 0%

profile of v1, /device:TPU:1, one launch (start us, length us, event | category | flops | bytes accessed | tf_op | source)
XLA Modules:
  0.0 145.9 jit_solution(6816060383106536188)
XLA Ops:
  0.1 0.7 slice.204
  2.6 6.4 %all-to-all-start = ((bf16[4,4,1536]{2,1,0:T(4,128)(2,1)}), bf16[4,4,1536]{2,1,0:T(4,128)(2,1)S(1)}, u32[]{:S(2)}, u32[]{:S(2)}) async-start(bf16[4,4,1536]{2,1,0:T(4,128)(2,1)} %broadcast_in_dim.113), calls=%async_computation | async-start | bytes 98304 | tf_op jit(solution)/shard_map/all_to_all | solution.py:33
  9.1 8.8 %collective-permute-start.1 = (bf16[2,128,128]{2,1,0:T(8,128)(2,1)}, bf16[2,128,128]{2,1,0:T(8,128)(2,1)S(1)}, u32[]{:S(2)}, u32[]{:S(2)}) collective-permute-start(bf16[2,128,128]{2,1,0:T(8,128)(2,1)} %param.13), channel_id=1, source_target_pairs={{0,1},{1,0},{2,3},{3,2},{4,5},{5,4},{6,7},{7,6},{8,9},{9,8},{10,11... | collective-permute-start | bytes 196616 | tf_op jit(solution)/shard_map/ppermute | solution.py:128
  17.9 2.0 %fusion.18 = bf16[128,512]{0,1:T(8,128)(2,1)} fusion(pred[512,512]{1,0:T(32,128)(4,1)S(1)} %fusion.29, bf16[2,128,512]{2,1,0:T(8,128)(2,1)} %param.7), kind=kOutput, calls=%fused_computation.52 | convolution fusion | flops 67436544 | bytes 524288 | tf_op jit(solution)/shard_map/dot_general | solution.py:15
  19.9 1.1 fusion.17
  21.4 2.0 %fusion.40 = (pred[128,1152]{0,1:T(8,128)(4,1)}, pred[128,1152]{0,1:T(8,128)(4,1)}) fusion(s32[1152]{0:T(1024)S(1)} %iota_add_fusion, pred[1152]{0:T(1024)(128)(4,1)S(1)} %get-tuple-element.31, pred[1152]{0:T(1024)(128)(4,1)S(1)} %get-tuple-element.30), kind=kLoop, calls=%fused_computation.83 | loop fusion | flops 884736 | bytes 301824 | tf_op jit(solution)/shard_map/and | solution.py:191
  23.5 5.4 %collective-permute-start.2 = (bf16[1,2,2,128,128]{4,3,2,1,0:T(8,128)(2,1)S(1)}, bf16[1,2,2,128,128]{4,3,2,1,0:T(8,128)(2,1)S(1)}, u32[]{:S(2)}, u32[]{:S(2)}) collective-permute-start(bf16[1,2,2,128,128]{4,3,2,1,0:T(8,128)(2,1)S(1)} %fusion.106), channel_id=1, source_target_pairs={{0,4},{4,8},{8,12},{12,16},{16,20},{20,24},{24,28},{28,32},{32,36}... | collective-permute-start | bytes 393224 | tf_op jit(solution)/shard_map/ppermute | solution.py:123
  28.8 3.1 %collective-permute-start.3 = (bf16[1,2,2,128,128]{4,3,2,1,0:T(8,128)(2,1)S(1)}, bf16[1,2,2,128,128]{4,3,2,1,0:T(8,128)(2,1)S(1)}, u32[]{:S(2)}, u32[]{:S(2)}) collective-permute-start(bf16[1,2,2,128,128]{4,3,2,1,0:T(8,128)(2,1)S(1)} %fusion.106), channel_id=1, source_target_pairs={{0,8},{4,12},{8,16},{12,20},{16,24},{20,28},{24,32},{28,36},{32,40... | collective-permute-start | bytes 393224 | tf_op jit(solution)/shard_map/ppermute | solution.py:123
  32.0 1.0 broadcast_in_dim.115
  33.0 5.8 %all-to-all-start.1 = ((bf16[16,16,1536]{2,1,0:T(8,128)(2,1)}), bf16[16,16,1536]{2,1,0:T(8,128)(2,1)S(1)}, u32[]{:S(2)}, u32[]{:S(2)}) async-start(bf16[16,16,1536]{2,1,0:T(8,128)(2,1)} %broadcast_in_dim.115), calls=%async_computation.1 | async-start | bytes 1572864 | tf_op jit(solution)/shard_map/all_to_all | solution.py:33
  38.9 1.8 %collective-permute-done.3 = bf16[1,2,2,128,128]{4,3,2,1,0:T(8,128)(2,1)S(1)} collective-permute-done((bf16[1,2,2,128,128]{4,3,2,1,0:T(8,128)(2,1)S(1)}, bf16[1,2,2,128,128]{4,3,2,1,0:T(8,128)(2,1)S(1)}, u32[]{:S(2)}, u32[]{:S(2)}) %collective-permute-start.3) | collective-permute-done | bytes 131104 | tf_op jit(solution)/shard_map/ppermute | solution.py:123
  40.7 2.7 %collective-permute-start.4 = (bf16[3,2,2,128,128]{4,3,2,1,0:T(8,128)(2,1)S(1)}, bf16[3,2,2,128,128]{4,3,2,1,0:T(8,128)(2,1)S(1)}, u32[]{:S(2)}, u32[]{:S(2)}) collective-permute-start(bf16[3,2,2,128,128]{4,3,2,1,0:T(8,128)(2,1)S(1)} %pad_maximum_fusion.1), channel_id=1, source_target_pairs={{0,24},{4,28},{8,32},{12,36},{16,40},{20,44},{24,48},{28,52},{32,5... | collective-permute-start | bytes 1179656 | tf_op jit(solution)/shard_map/ppermute | solution.py:123
  43.4 3.4 %collective-permute-start.5 = (bf16[3,2,2,128,128]{4,3,2,1,0:T(8,128)(2,1)S(1)}, bf16[3,2,2,128,128]{4,3,2,1,0:T(8,128)(2,1)S(1)}, u32[]{:S(2)}, u32[]{:S(2)}) collective-permute-start(bf16[3,2,2,128,128]{4,3,2,1,0:T(8,128)(2,1)S(1)} %pad_maximum_fusion.1), channel_id=1, source_target_pairs={{0,12},{4,16},{8,20},{12,24},{16,28},{20,32},{24,36},{28,40},{32,4... | collective-permute-start | bytes 1179656 | tf_op jit(solution)/shard_map/ppermute | solution.py:123
  48.1 12.4 %collective-permute-done.4 = bf16[3,2,2,128,128]{4,3,2,1,0:T(8,128)(2,1)S(1)} collective-permute-done((bf16[3,2,2,128,128]{4,3,2,1,0:T(8,128)(2,1)S(1)}, bf16[3,2,2,128,128]{4,3,2,1,0:T(8,128)(2,1)S(1)}, u32[]{:S(2)}, u32[]{:S(2)}) %collective-permute-start.4) | collective-permute-done | bytes 393248 | tf_op jit(solution)/shard_map/ppermute | solution.py:123
  60.5 8.6 %collective-permute-done.5 = bf16[3,2,2,128,128]{4,3,2,1,0:T(8,128)(2,1)S(1)} collective-permute-done((bf16[3,2,2,128,128]{4,3,2,1,0:T(8,128)(2,1)S(1)}, bf16[3,2,2,128,128]{4,3,2,1,0:T(8,128)(2,1)S(1)}, u32[]{:S(2)}, u32[]{:S(2)}) %collective-permute-start.5) | collective-permute-done | bytes 393248 | tf_op jit(solution)/shard_map/ppermute | solution.py:123
  73.2 1.9 %collective-permute-start = (bf16[256,1536]{1,0:T(8,128)(2,1)S(1)}, bf16[256,1536]{1,0:T(8,128)(2,1)S(1)}, u32[]{:S(2)}, u32[]{:S(2)}) collective-permute-start(bf16[256,1536]{1,0:T(8,128)(2,1)S(1)} %bitcast.217), channel_id=1, source_target_pairs={{0,4},{4,0},{1,5},{5,1},{2,6},{6,2},{3,7},{7,3},{8,12},{12,8},{9,1... | collective-permute-start | bytes 2359304 | tf_op jit(solution)/shard_map/ppermute | solution.py:42
  79.2 2.0 %collective-permute-start.6 = (bf16[256,1536]{1,0:T(8,128)(2,1)S(1)}, bf16[256,1536]{1,0:T(8,128)(2,1)S(1)}, u32[]{:S(2)}, u32[]{:S(2)}) collective-permute-start(bf16[256,1536]{1,0:T(8,128)(2,1)S(1)} %pad_maximum_fusion), channel_id=1, source_target_pairs={{0,4},{4,0},{1,5},{5,1},{2,6},{6,2},{3,7},{7,3},{8,12},{12,8},{9,1... | collective-permute-start | bytes 2359304 | tf_op jit(solution)/shard_map/ppermute | solution.py:42
  82.6 0.7 collective-permute-done.6
  83.4 1.1 fusion.10
  84.5 3.7 %all-to-all-start.2 = ((bf16[16,16,1536]{2,1,0:T(8,128)(2,1)}), bf16[16,16,1536]{2,1,0:T(8,128)(2,1)S(1)}, u32[]{:S(2)}, u32[]{:S(2)}) async-start(bf16[16,16,1536]{2,1,0:T(8,128)(2,1)} %bitcast.39), calls=%async_computation.2 | async-start | bytes 1572864 | tf_op jit(solution)/shard_map/all_to_all | solution.py:33
  91.0 11.3 %all-to-all-done.2 = bf16[16,16,1536]{2,1,0:T(8,128)(2,1)S(1)} async-done(((bf16[16,16,1536]{2,1,0:T(8,128)(2,1)}), bf16[16,16,1536]{2,1,0:T(8,128)(2,1)S(1)}, u32[]{:S(2)}, u32[]{:S(2)}) %all-to-all-start.2) | async-done | bytes 786464 | tf_op jit(solution)/shard_map/all_to_all | solution.py:33
  103.1 3.4 %all-to-all-start.3 = ((bf16[4,16,1536]{2,1,0:T(8,128)(2,1)}), bf16[4,16,1536]{2,1,0:T(8,128)(2,1)S(1)}, u32[]{:S(2)}, u32[]{:S(2)}) async-start(bf16[4,16,1536]{2,1,0:T(8,128)(2,1)} %broadcast_in_dim.134), calls=%async_computation.3 | async-start | bytes 393216 | tf_op jit(solution)/shard_map/all_to_all | solution.py:33
  107.3 4.3 %all-to-all-done.3 = bf16[4,16,1536]{2,1,0:T(8,128)(2,1)S(1)} async-done(((bf16[4,16,1536]{2,1,0:T(8,128)(2,1)}), bf16[4,16,1536]{2,1,0:T(8,128)(2,1)S(1)}, u32[]{:S(2)}, u32[]{:S(2)}) %all-to-all-start.3) | async-done | bytes 196640 | tf_op jit(solution)/shard_map/all_to_all | solution.py:33
  112.0 1.0 broadcast_in_dim.135
  113.0 3.6 %all-to-all-start.4 = ((bf16[16,16,1536]{2,1,0:T(8,128)(2,1)}), bf16[16,16,1536]{2,1,0:T(8,128)(2,1)S(1)}, u32[]{:S(2)}, u32[]{:S(2)}) async-start(bf16[16,16,1536]{2,1,0:T(8,128)(2,1)} %broadcast_in_dim.135), calls=%async_computation.4 | async-start | bytes 1572864 | tf_op jit(solution)/shard_map/all_to_all | solution.py:33
  117.4 10.2 %all-to-all-done.4 = bf16[16,16,1536]{2,1,0:T(8,128)(2,1)S(1)} async-done(((bf16[16,16,1536]{2,1,0:T(8,128)(2,1)}), bf16[16,16,1536]{2,1,0:T(8,128)(2,1)S(1)}, u32[]{:S(2)}, u32[]{:S(2)}) %all-to-all-start.4) | async-done | bytes 786464 | tf_op jit(solution)/shard_map/all_to_all | solution.py:33
  127.6 6.5 %collective-permute-start.7 = (bf16[256,1536]{1,0:T(8,128)(2,1)S(1)}, bf16[256,1536]{1,0:T(8,128)(2,1)S(1)}, u32[]{:S(2)}, u32[]{:S(2)}) collective-permute-start(bf16[256,1536]{1,0:T(8,128)(2,1)S(1)} %bitcast.224), channel_id=1, source_target_pairs={{0,4},{4,0},{1,5},{5,1},{2,6},{6,2},{3,7},{7,3},{8,12},{12,8},{9,1... | collective-permute-start | bytes 2359304 | tf_op jit(solution)/shard_map/ppermute | solution.py:42
  134.1 1.9 %fusion.164 = f32[4,128]{1,0:T(4,128)S(1)} fusion(pred[128,1152]{0,1:T(8,128)(4,1)S(1)} %copy-done.11, bf16[2,2,1152,128]{3,2,1,0:T(8,128)(2,1)} %fusion.105, f32[512]{0:T(512)S(1)} %copy-done.13, f32[128,512]{1,0:T(8,128)S(1)} %get-tuple-element.27, f32[128]{0:T(128)S(1)} %add_rsqrt_fusion.1), kind=kOutput, calls=%fused_computation.254 | convolution fusion | flops 153552000 | bytes 709120 | tf_op jit(solution)/shard_map/sub | solution.py:115
  136.1 2.4 %fusion.11 = f32[128,4,128]{2,0,1:T(8,128)S(1)} fusion(f32[4,128]{1,0:T(4,128)S(1)} %fusion.164, bf16[2,2,1152,128]{3,2,1,0:T(8,128)(2,1)} %fusion.105, pred[128,1152]{0,1:T(8,128)(4,1)S(1)} %copy-done.11, f32[512]{0:T(512)S(1)} %copy-done.13, f32[128,512]{1,0:T(8,128)S(1)} %get-tuple-element.27, f32[128]{0:T(128)S(1)} %add_rsqrt_fusion.1), kind=kOutput, calls=%fused_computation.34 | convolution fusion | flops 305137280 | bytes 1266176 | tf_op jit(solution)/shard_map/hqk,kd->qhd/dot_general | solution.py:117
  140.7 1.9 %fusion.167 = f32[4,128]{1,0:T(4,128)S(1)} fusion(pred[128,1152]{0,1:T(8,128)(4,1)S(1)} %copy-done.10, bf16[2,2,1152,128]{3,2,1,0:T(8,128)(2,1)} %fusion.105, bf16[16,4,8,128]{3,2,1,0:T(8,128)(2,1)S(1)} %get-tuple-element.25), kind=kOutput, calls=%fused_computation.255 | convolution fusion | flops 153355392 | bytes 575488 | tf_op jit(solution)/shard_map/sub | solution.py:115
  142.5 2.3 %fusion.12 = f32[128,4,128]{2,0,1:T(8,128)S(1)} fusion(f32[4,128]{1,0:T(4,128)S(1)} %fusion.167, bf16[2,2,1152,128]{3,2,1,0:T(8,128)(2,1)} %fusion.105, pred[128,1152]{0,1:T(8,128)(4,1)S(1)} %copy-done.10, bf16[16,4,8,128]{3,2,1,0:T(8,128)(2,1)S(1)} %get-tuple-element.25), kind=kOutput, calls=%fused_computation.35 | convolution fusion | flops 304940672 | bytes 1132544 | tf_op jit(solution)/shard_map/hqk,kd->qhd/dot_general | solution.py:117
  145.1 0.7 pad_maximum_fusion.3
  (123 shorter events, 21.2 us)
Async XLA Ops:
  0.0 19.9 %copy-start.14 = (bf16[2,128,512]{2,1,0:T(8,128)(2,1)S(1)}, bf16[2,128,512]{2,1,0:T(8,128)(2,1)}, u32[]{:S(2)}) copy-start(bf16[2,128,512]{2,1,0:T(8,128)(2,1)} %param.7) | copy-start | bytes 786436
  1.7 19.2 %copy-start.15 = (bf16[2,128,512]{2,1,0:T(8,128)(2,1)S(1)}, bf16[2,128,512]{2,1,0:T(8,128)(2,1)}, u32[]{:S(2)}) copy-start(bf16[2,128,512]{2,1,0:T(8,128)(2,1)} %param.8) | copy-start | bytes 786436
  2.6 29.3 %all-to-all-start = ((bf16[4,4,1536]{2,1,0:T(4,128)(2,1)}), bf16[4,4,1536]{2,1,0:T(4,128)(2,1)S(1)}, u32[]{:S(2)}, u32[]{:S(2)}) async-start(bf16[4,4,1536]{2,1,0:T(4,128)(2,1)} %broadcast_in_dim.113), calls=%async_computation | async-start | bytes 98304 | tf_op jit(solution)/shard_map/all_to_all | solution.py:33
  9.1 14.3 %collective-permute-start.1 = (bf16[2,128,128]{2,1,0:T(8,128)(2,1)}, bf16[2,128,128]{2,1,0:T(8,128)(2,1)S(1)}, u32[]{:S(2)}, u32[]{:S(2)}) collective-permute-start(bf16[2,128,128]{2,1,0:T(8,128)(2,1)} %param.13), channel_id=1, source_target_pairs={{0,1},{1,0},{2,3},{3,2},{4,5},{5,4},{6,7},{7,6},{8,9},{9,8},{10,11... | collective-permute-start | bytes 196616 | tf_op jit(solution)/shard_map/ppermute | solution.py:128
  19.9 3.5 %copy-start.12 = (bf16[2,128,128]{2,1,0:T(8,128)(2,1)S(1)}, bf16[2,128,128]{2,1,0:T(8,128)(2,1)}, u32[]{:S(2)}) copy-start(bf16[2,128,128]{2,1,0:T(8,128)(2,1)} %param.13) | copy-start | bytes 196612
  20.9 11.0 %copy-start.16 = (f32[2,128,1]{1,2,0:T(1,128)S(1)}, f32[2,128,1]{1,2,0:T(1,128)}, u32[]{:S(2)}) copy-start(f32[2,128,1]{1,2,0:T(1,128)} %param.10) | copy-start | bytes 3076
  23.5 15.4 %collective-permute-start.2 = (bf16[1,2,2,128,128]{4,3,2,1,0:T(8,128)(2,1)S(1)}, bf16[1,2,2,128,128]{4,3,2,1,0:T(8,128)(2,1)S(1)}, u32[]{:S(2)}, u32[]{:S(2)}) collective-permute-start(bf16[1,2,2,128,128]{4,3,2,1,0:T(8,128)(2,1)S(1)} %fusion.106), channel_id=1, source_target_pairs={{0,4},{4,8},{8,12},{12,16},{16,20},{20,24},{24,28},{28,32},{32,36}... | collective-permute-start | bytes 393224 | tf_op jit(solution)/shard_map/ppermute | solution.py:123
  28.8 11.8 %collective-permute-start.3 = (bf16[1,2,2,128,128]{4,3,2,1,0:T(8,128)(2,1)S(1)}, bf16[1,2,2,128,128]{4,3,2,1,0:T(8,128)(2,1)S(1)}, u32[]{:S(2)}, u32[]{:S(2)}) collective-permute-start(bf16[1,2,2,128,128]{4,3,2,1,0:T(8,128)(2,1)S(1)} %fusion.106), channel_id=1, source_target_pairs={{0,8},{4,12},{8,16},{12,20},{16,24},{20,28},{24,32},{28,36},{32,40... | collective-permute-start | bytes 393224 | tf_op jit(solution)/shard_map/ppermute | solution.py:123
  32.0 1.0 copy-start.1
  33.0 40.2 %all-to-all-start.1 = ((bf16[16,16,1536]{2,1,0:T(8,128)(2,1)}), bf16[16,16,1536]{2,1,0:T(8,128)(2,1)S(1)}, u32[]{:S(2)}, u32[]{:S(2)}) async-start(bf16[16,16,1536]{2,1,0:T(8,128)(2,1)} %broadcast_in_dim.115), calls=%async_computation.1 | async-start | bytes 1572864 | tf_op jit(solution)/shard_map/all_to_all | solution.py:33
  40.7 19.8 %collective-permute-start.4 = (bf16[3,2,2,128,128]{4,3,2,1,0:T(8,128)(2,1)S(1)}, bf16[3,2,2,128,128]{4,3,2,1,0:T(8,128)(2,1)S(1)}, u32[]{:S(2)}, u32[]{:S(2)}) collective-permute-start(bf16[3,2,2,128,128]{4,3,2,1,0:T(8,128)(2,1)S(1)} %pad_maximum_fusion.1), channel_id=1, source_target_pairs={{0,24},{4,28},{8,32},{12,36},{16,40},{20,44},{24,48},{28,52},{32,5... | collective-permute-start | bytes 1179656 | tf_op jit(solution)/shard_map/ppermute | solution.py:123
  43.4 25.7 %collective-permute-start.5 = (bf16[3,2,2,128,128]{4,3,2,1,0:T(8,128)(2,1)S(1)}, bf16[3,2,2,128,128]{4,3,2,1,0:T(8,128)(2,1)S(1)}, u32[]{:S(2)}, u32[]{:S(2)}) collective-permute-start(bf16[3,2,2,128,128]{4,3,2,1,0:T(8,128)(2,1)S(1)} %pad_maximum_fusion.1), channel_id=1, source_target_pairs={{0,12},{4,16},{8,20},{12,24},{16,28},{20,32},{24,36},{28,40},{32,4... | collective-permute-start | bytes 1179656 | tf_op jit(solution)/shard_map/ppermute | solution.py:123
  69.8 6.1 %copy-start = (bf16[2,128,512]{2,1,0:T(8,128)(2,1)S(1)}, bf16[2,128,512]{2,1,0:T(8,128)(2,1)}, u32[]{:S(2)}) copy-start(bf16[2,128,512]{2,1,0:T(8,128)(2,1)} %param.9) | copy-start | bytes 786436
  70.4 4.7 %copy-start.9 = (bf16[2,128,128]{2,1,0:T(8,128)(2,1)S(1)}, bf16[2,128,128]{2,1,0:T(8,128)(2,1)}, u32[]{:S(2)}) copy-start(bf16[2,128,128]{2,1,0:T(8,128)(2,1)} %get-tuple-element.34) | copy-start | bytes 196612
  73.2 4.2 %collective-permute-start = (bf16[256,1536]{1,0:T(8,128)(2,1)S(1)}, bf16[256,1536]{1,0:T(8,128)(2,1)S(1)}, u32[]{:S(2)}, u32[]{:S(2)}) collective-permute-start(bf16[256,1536]{1,0:T(8,128)(2,1)S(1)} %bitcast.217), channel_id=1, source_target_pairs={{0,4},{4,0},{1,5},{5,1},{2,6},{6,2},{3,7},{7,3},{8,12},{12,8},{9,1... | collective-permute-start | bytes 2359304 | tf_op jit(solution)/shard_map/ppermute | solution.py:42
  78.6 2.7 %copy-start.3 = (bf16[2,2,128,128]{3,2,1,0:T(8,128)(2,1)S(1)}, bf16[2,2,128,128]{3,2,1,0:T(8,128)(2,1)}, u32[]{:S(2)}) copy-start(bf16[2,2,128,128]{3,2,1,0:T(8,128)(2,1)} %get-tuple-element.10) | copy-start | bytes 393220
  79.2 4.2 %collective-permute-start.6 = (bf16[256,1536]{1,0:T(8,128)(2,1)S(1)}, bf16[256,1536]{1,0:T(8,128)(2,1)S(1)}, u32[]{:S(2)}, u32[]{:S(2)}) collective-permute-start(bf16[256,1536]{1,0:T(8,128)(2,1)S(1)} %pad_maximum_fusion), channel_id=1, source_target_pairs={{0,4},{4,0},{1,5},{5,1},{2,6},{6,2},{3,7},{7,3},{8,12},{12,8},{9,1... | collective-permute-start | bytes 2359304 | tf_op jit(solution)/shard_map/ppermute | solution.py:42
  84.5 3.8 %copy-start.8 = (bf16[2,128,128]{2,1,0:T(8,128)(2,1)S(1)}, bf16[2,128,128]{2,1,0:T(8,128)(2,1)}, u32[]{:S(2)}) copy-start(bf16[2,128,128]{2,1,0:T(8,128)(2,1)} %slice_bitcast_fusion.32) | copy-start | bytes 196612
  84.5 4.5 %copy-start.7 = (bf16[2,128,128]{2,1,0:T(8,128)(2,1)S(1)}, bf16[2,128,128]{2,1,0:T(8,128)(2,1)}, u32[]{:S(2)}) copy-start(bf16[2,128,128]{2,1,0:T(8,128)(2,1)} %slice_bitcast_fusion.31) | copy-start | bytes 196612
  84.5 5.2 %copy-start.6 = (bf16[2,128,128]{2,1,0:T(8,128)(2,1)S(1)}, bf16[2,128,128]{2,1,0:T(8,128)(2,1)}, u32[]{:S(2)}) copy-start(bf16[2,128,128]{2,1,0:T(8,128)(2,1)} %slice_bitcast_fusion.30) | copy-start | bytes 196612
  84.5 17.8 %all-to-all-start.2 = ((bf16[16,16,1536]{2,1,0:T(8,128)(2,1)}), bf16[16,16,1536]{2,1,0:T(8,128)(2,1)S(1)}, u32[]{:S(2)}, u32[]{:S(2)}) async-start(bf16[16,16,1536]{2,1,0:T(8,128)(2,1)} %bitcast.39), calls=%async_computation.2 | async-start | bytes 1572864 | tf_op jit(solution)/shard_map/all_to_all | solution.py:33
  88.9 17.5 %copy-start.5 = (bf16[128,512]{0,1:T(8,128)(2,1)S(1)}, bf16[128,512]{0,1:T(8,128)(2,1)}, u32[]{:S(2)}) copy-start(bf16[128,512]{0,1:T(8,128)(2,1)} %fusion.17) | copy-start | bytes 393220
  103.1 8.5 %all-to-all-start.3 = ((bf16[4,16,1536]{2,1,0:T(8,128)(2,1)}), bf16[4,16,1536]{2,1,0:T(8,128)(2,1)S(1)}, u32[]{:S(2)}, u32[]{:S(2)}) async-start(bf16[4,16,1536]{2,1,0:T(8,128)(2,1)} %broadcast_in_dim.134), calls=%async_computation.3 | async-start | bytes 393216 | tf_op jit(solution)/shard_map/all_to_all | solution.py:33
  106.7 5.3 %copy-start.2 = (bf16[16,1536]{1,0:T(8,128)(2,1)S(1)}, bf16[16,1536]{1,0:T(8,128)(2,1)}, u32[]{:S(2)}) copy-start(bf16[16,1536]{1,0:T(8,128)(2,1)} %copy-done.1) | copy-start | bytes 147460
  113.0 14.6 %all-to-all-start.4 = ((bf16[16,16,1536]{2,1,0:T(8,128)(2,1)}), bf16[16,16,1536]{2,1,0:T(8,128)(2,1)S(1)}, u32[]{:S(2)}, u32[]{:S(2)}) async-start(bf16[16,16,1536]{2,1,0:T(8,128)(2,1)} %broadcast_in_dim.135), calls=%async_computation.4 | async-start | bytes 1572864 | tf_op jit(solution)/shard_map/all_to_all | solution.py:33
  116.6 17.5 %copy-start.11 = (pred[128,1152]{0,1:T(8,128)(4,1)S(1)}, pred[128,1152]{0,1:T(8,128)(4,1)}, u32[]{:S(2)}) copy-start(pred[128,1152]{0,1:T(8,128)(4,1)} %get-tuple-element.22) | copy-start | bytes 442372
  116.6 17.5 %copy-start.13 = (f32[512]{0:T(512)S(1)}, f32[512]{0:T(512)}, u32[]{:S(2)}) copy-start(f32[512]{0:T(512)} %param.12) | copy-start | bytes 6148
  127.6 11.6 %collective-permute-start.7 = (bf16[256,1536]{1,0:T(8,128)(2,1)S(1)}, bf16[256,1536]{1,0:T(8,128)(2,1)S(1)}, u32[]{:S(2)}, u32[]{:S(2)}) collective-permute-start(bf16[256,1536]{1,0:T(8,128)(2,1)S(1)} %bitcast.224), channel_id=1, source_target_pairs={{0,4},{4,0},{1,5},{5,1},{2,6},{6,2},{3,7},{7,3},{8,12},{12,8},{9,1... | collective-permute-start | bytes 2359304 | tf_op jit(solution)/shard_map/ppermute | solution.py:42
  136.0 2.6 %copy-start.4 = (bf16[128,512]{0,1:T(8,128)(2,1)S(1)}, bf16[128,512]{0,1:T(8,128)(2,1)}, u32[]{:S(2)}) copy-start(bf16[128,512]{0,1:T(8,128)(2,1)} %fusion.18) | copy-start | bytes 393220
  139.8 0.9 copy-start.10
